TPU v7x, 32 devices: a whole 2x2x4 slice. The times are simulated.
32 devices in a mesh: rep: 2 (over x), seq: 8 (over z, y), head: 2 (over core).
Axes of the slice: x: 2, y: 2, z: 4, core: 2. Of those that a mesh axis runs over, the one named last changes fastest.
Arguments:
- query_rows: bfloat16 [2048, 4096], P(('rep', 'seq'), 'head'), parts along dimension 0, may hold values from -40 to 40
- key_rows: bfloat16 [2048, 4096], P(('rep', 'seq'), 'head'), parts along dimension 0, may hold values from -6 to 6
- value_rows: bfloat16 [2048, 4096], P(('rep', 'seq'), 'head'), parts along dimension 0, may hold values from -6 to 6
- rand_blocks: int32 [16, 32, 3], P('rep'), parts along dimension 0, may hold values from 0 to 7, as said below
- out_weight: bfloat16 [4096, 4096], P('seq', 'head'), may hold values from -0.09375 to 0.09375
Outputs:
- projected: bfloat16 [2048, 4096], P(('rep', 'seq'), 'head'), parts along dimension 0
There are 2 independent parts, one for each index of `rep`. A program takes and returns all parts, laid end to end along the dimension named above; an argument that names none is the same for every part. Nothing has to cross between parts.
Inputs may be any that keep to these rules, and one draw needn't show every extreme that they name: `rand_blocks`: each entry is uniform over the blocks of the whole sequence. For the query blocks of one index of seq and the heads of one index of head, at most 6 entries name blocks held by one index of seq, and in every draw some index of seq is named exactly 6 times.
All inputs are finite; a program needn't handle non-finite values.
Results may differ from a plain program's by a relative error of at most 0.008.
Values may be sent and summed in bfloat16 or wider, within the bound.
No kernel may reach another device: no remote copies, remote signals or barrier semaphores. Data moves between devices by JAX's collectives and lax.ppermute only.
A program may use at most 128 MiB of HBM per device.

v0:
```python
import math
import jax
import jax.numpy as jnp
from jax import lax
from jax.sharding import PartitionSpec as P

HD = 128
BLK = 128
R = 3


def broadcast(block, axis, owner):
    block = jnp.where(lax.axis_index(axis) == owner, block, jnp.zeros_like(block))
    return lax.psum(block, axis)


def padded(array, sides, width):
    for axis, dim in sides:
        peers, length = (lax.axis_size(axis), array.shape[dim])
        up = [(i, (i + 1) % peers) for i in range(peers - 1)]
        down = [(j, i) for i, j in up]
        last = lax.slice_in_dim(array, length - width, length, axis=dim)
        initial = lax.slice_in_dim(array, 0, width, axis=dim)
        before = lax.ppermute(last, axis, up)
        after = lax.ppermute(initial, axis, down)
        array = jnp.concatenate([before, array, after], axis=dim)
    return array


def masked_softmax(scores, allowed):
    masked = jnp.where(allowed, scores, -jnp.inf)
    row_peak = jnp.max(masked, axis=-1, keepdims=True)
    expon_terms = jnp.where(allowed, jnp.exp(masked - row_peak), 0.0)
    return expon_terms / jnp.sum(expon_terms, axis=-1, keepdims=True)


def share_block(stacked, root_index):
    return broadcast(stacked, "seq", root_index)


def local(query_rows, key_rows, value_rows, rand_blocks, out_weight):
    tokens, features = query_rows.shape
    head_width = HD
    head_count = features // head_width
    blocks = tokens // BLK
    seq_count = lax.axis_size("seq")
    seq_index = lax.axis_index("seq")
    head_index = lax.axis_index("head")
    block_total = blocks * seq_count
    score_scale = 1.0 / math.sqrt(head_width)
    request_count = blocks * head_count * R
    slot_depth = (request_count + seq_count - 1) // seq_count
    first_rows = jnp.stack((query_rows, key_rows, value_rows))
    final_rows = jnp.stack((query_rows, key_rows, value_rows))
    first_glob = share_block(first_rows, 0)
    final_glob = share_block(final_rows, seq_count - 1)
    paired = jnp.stack((key_rows, value_rows))
    extended = padded(paired, (("seq", 1),), BLK)
    ext_heads = extended.reshape(2, blocks + 2, BLK, head_count, head_width).transpose(
        0, 3, 1, 2, 4
    )
    group_table = lax.dynamic_slice_in_dim(rand_blocks, head_index * head_count, head_count, 1)
    all_requests = group_table.reshape(seq_count, request_count)
    all_owner = all_requests // blocks
    request_order = jnp.arange(request_count, dtype=jnp.int32)
    earlier_request = request_order[None, :] < request_order[:, None]
    same_owner = all_owner[:, :, None] == all_owner[:, None, :]
    all_position = jnp.sum(same_owner & earlier_request[None], axis=2)
    owned_here = all_owner == seq_index
    slot_range = jnp.arange(slot_depth, dtype=jnp.int32)
    picked = owned_here[:, None, :] & (all_position[:, None, :] == slot_range[None, :, None])
    picked_request = jnp.sum(jnp.where(picked, request_order[None, None, :], 0), axis=2)
    picked_block = jnp.take_along_axis(all_requests, picked_request, axis=1) - seq_index * blocks
    picked_block = jnp.clip(picked_block, 0, blocks - 1).reshape(-1)
    picked_head = (picked_request // R % head_count).reshape(-1)
    local_pairs = paired.reshape(2, blocks, BLK, head_count, head_width)
    outgoing = local_pairs[:, picked_block, :, picked_head, :]
    outgoing = outgoing.reshape(seq_count, slot_depth, 2, BLK, head_width)
    received = lax.all_to_all(outgoing, "seq", split_axis=0, concat_axis=0, tiled=True)
    my_requests = lax.dynamic_slice_in_dim(all_requests, seq_index, 1, 0)[0]
    my_position = lax.dynamic_slice_in_dim(all_position, seq_index, 1, 0)[0]
    my_owner = my_requests // blocks
    rand_pairs = jnp.take(
        received.reshape(seq_count * slot_depth, 2, BLK, head_width),
        my_owner * slot_depth + my_position,
        axis=0,
    )
    rand_pairs = rand_pairs.reshape(blocks, head_count, R, 2, BLK, head_width).transpose(
        3, 1, 0, 2, 4, 5
    )
    block_ids = seq_index * blocks + jnp.arange(blocks, dtype=jnp.int32)
    base_slots = jnp.stack(
        [
            jnp.zeros((blocks,), jnp.int32),
            jnp.full((blocks,), block_total - 1, jnp.int32),
            jnp.clip(block_ids - 1, 0, block_total - 1),
            block_ids,
            jnp.clip(block_ids + 1, 0, block_total - 1),
        ],
        axis=1,
    )
    my_table = my_requests.reshape(blocks, head_count, R).transpose(1, 0, 2)
    slot_ids = jnp.concatenate(
        [jnp.broadcast_to(base_slots[None], (head_count, blocks, 5)), my_table], axis=2
    )
    slot_count = slot_ids.shape[2]
    equal_pair = slot_ids[:, :, :, None] == slot_ids[:, :, None, :]
    earlier = jnp.arange(slot_count)[None, :] < jnp.arange(slot_count)[:, None]
    slot_live = jnp.logical_not(jnp.any(equal_pair & earlier[None, None], axis=3))
    key_live = jnp.repeat(slot_live, BLK, axis=2)
    window_index = jnp.arange(blocks)[:, None] + jnp.arange(3)[None, :]
    query_heads = query_rows.reshape(blocks, BLK, head_count, head_width).transpose(2, 0, 1, 3)
    first_heads = first_glob.reshape(3, BLK, head_count, head_width).transpose(0, 2, 1, 3)
    final_heads = final_glob.reshape(3, BLK, head_count, head_width).transpose(0, 2, 1, 3)
    target_heads = max(1, 512 // (blocks * BLK))
    heads_step = max(
        (
            width
            for width in range(1, head_count + 1)
            if head_count % width == 0 and width <= target_heads
        )
    )

    def collect(ext_part, first_block, final_block, rand_part):
        steps_here = ext_part.shape[0]
        window_blocks = ext_part[:, window_index]
        glob_blocks = jnp.stack((first_block, final_block), axis=1)[:, None]
        joined = jnp.concatenate([glob_blocks, window_blocks, rand_part], axis=2)
        return joined.reshape(steps_here, blocks, slot_count * BLK, head_width)

    def attend(head_items):
        (
            query_one,
            key_ext,
            value_ext,
            key_first,
            value_first,
            key_final,
            value_final,
            key_rand,
            value_rand,
            live_one,
        ) = head_items
        keys_sel = collect(key_ext, key_first, key_final, key_rand)
        values_sel = collect(value_ext, value_first, value_final, value_rand)
        scores = (
            jnp.einsum("hibd,hikd->hibk", query_one, keys_sel, preferred_element_type=jnp.float32)
            * score_scale
        )
        weights = masked_softmax(scores, live_one[:, :, None, :]).astype(jnp.bfloat16)
        mixed = jnp.einsum(
            "hibk,hikd->hibd", weights, values_sel, preferred_element_type=jnp.float32
        )
        return mixed.astype(jnp.bfloat16)

    def split_heads(array):
        return array.reshape((head_count // heads_step, heads_step) + array.shape[1:])

    head_inputs = (
        query_heads,
        ext_heads[0],
        ext_heads[1],
        first_heads[1],
        first_heads[2],
        final_heads[1],
        final_heads[2],
        rand_pairs[0],
        rand_pairs[1],
        key_live,
    )
    block_heads = lax.map(attend, tuple((split_heads(item) for item in head_inputs)))
    block_heads = block_heads.reshape(head_count, blocks, BLK, head_width)
    attended = block_heads.transpose(1, 2, 0, 3).reshape(tokens, features)
    glob_query = jnp.concatenate((first_glob[0], final_glob[0]), axis=0).reshape(
        2 * BLK, head_count, head_width
    )
    key_heads = key_rows.reshape(tokens, head_count, head_width)
    value_wide = value_rows.reshape(tokens, head_count, head_width).astype(jnp.float32)
    glob_scores = (
        jnp.einsum("rhd,thd->hrt", glob_query, key_heads, preferred_element_type=jnp.float32)
        * score_scale
    )
    local_peak = jnp.max(glob_scores, axis=2)
    row_peak = lax.pmax(local_peak, "seq")
    expon_terms = jnp.exp(glob_scores - row_peak[:, :, None])
    denoms = jnp.sum(expon_terms, axis=2)
    numer_terms = jnp.einsum(
        "hrt,thd->hrd", expon_terms, value_wide, preferred_element_type=jnp.float32
    )
    numer_terms, denoms = lax.psum((numer_terms, denoms), "seq")
    glob_out = (
        (numer_terms / denoms[:, :, None])
        .astype(jnp.bfloat16)
        .transpose(1, 0, 2)
        .reshape(2 * BLK, features)
    )
    head_block = jnp.where(seq_index == 0, glob_out[:BLK], attended)
    attended = attended.at[:BLK].set(head_block)
    tail_block = jnp.where(seq_index == seq_count - 1, glob_out[BLK:], attended)
    attended = attended.at[tokens - BLK :].set(tail_block)
    partial_terms = lax.dot_general(
        lax.all_gather(out_weight, "seq", axis=0, tiled=True),
        attended,
        (((1,), (1,)), ((), ())),
        preferred_element_type=jnp.float32,
    )
    summed = lax.psum_scatter(
        partial_terms.astype(jnp.bfloat16), "head", scatter_dimension=0, tiled=True
    ).astype(jnp.float32)
    return summed.T.astype(jnp.bfloat16)


def solution(mesh):
    placed = (
        P(("rep", "seq"), "head"),
        P(("rep", "seq"), "head"),
        P(("rep", "seq"), "head"),
        P("rep", None, None),
        P("seq", "head"),
    )
    return jax.shard_map(
        local, mesh=mesh, in_specs=placed, out_specs=P(("rep", "seq"), "head"), check_vma=False
    )
```

profile of v0, /device:TPU:0, one launch (start us, length us, event | category | flops | bytes accessed | tf_op | source)
XLA Modules:
  0.0 597.0 jit_solution(8939532959045065275)
XLA Ops:
  7.9 1.5 copy.85
  9.7 1.9 broadcast_select_fusion
  11.8 132.2 %all-reduce.6.cloned.1.call-done = (bf16[3,128,2048]{1,2,0:T(8,128)(2,1)}, bf16[3,128,2048]{1,2,0:T(8,128)(2,1)}) async-done(((bf16[3,128,2048]{1,2,0:T(8,128)(2,1)}, bf16[3,128,2048]{1,2,0:T(8,128)(2,1)}), (bf16[3,128,2048]{1,2,0:T(8,128)(2,1)}, bf16[3,128,2048]{1,2,0:T(8,128)(2,1)})) %all-reduce.6.cloned.1.call-update) | async-done | bytes 3145744 | tf_op jit(solution)/shard_map/psum | solution.py:14
  148.2 1.8 multiply_reduce_fusion
  150.0 35.1 %pmax.7 = f32[16,256]{1,0:T(8,128)S(1)} all-reduce(f32[16,256]{1,0:T(8,128)S(1)} %get-tuple-element.247), channel_id=1, replica_groups=mesh['rep'=2,'seq'=8,'head'=2] {'seq'}, use_global_device_ids=true, to_apply=%region_3.4 | all-reduce | flops 4096 | bytes 32768 | tf_op jit(solution)/shard_map/pmax | solution.py:184
  185.1 3.0 fusion.25
  194.4 2.8 gather_fusion.2
  197.2 4.6 all-to-all-start
  202.9 4.7 collective-permute-start
  213.0 35.9 %collective-permute-done = bf16[2,128,2048]{1,2,0:T(8,128)(2,1)} collective-permute-done((bf16[2,128,2048]{1,2,0:T(8,128)(2,1)}, bf16[2,128,2048]{1,2,0:T(8,128)(2,1)}, u32[]{:S(2)}, u32[]{:S(2)}) %collective-permute-start) | collective-permute-done | bytes 1048608 | tf_op jit(solution)/shard_map/ppermute | solution.py:24
  248.8 3.3 pad_maximum_fusion.2
  252.1 4.7 copy.100
  256.8 2.9 copy.128
  259.8 2.2 fusion.58
  263.1 2.1 fusion.59
  265.2 2.1 copy.99
  269.7 101.5 %psum.31 = f32[16,256]{1,0:T(8,128)S(1)} all-reduce(f32[16,256]{1,0:T(8,128)S(1)} %fusion.24), channel_id=1, replica_groups=mesh['rep'=2,'seq'=8,'head'=2] {'seq'}, use_global_device_ids=true, to_apply=%region_6.7 | all-reduce | flops 4096 | bytes 32768 | tf_op jit(solution)/shard_map/psum | solution.py:190
  371.2 1.9 fusion.32
  375.4 3.1 gather_fusion.3
  378.8 1.5 fusion.57
  380.3 49.2 %while.16 = (s32[]{:T(128)}, bf16[4,4,1,128,128]{3,4,1,0,2:T(8,128)(2,1)}, pred[4,4,1,1024]{3,1,2,0:T(4,128)(4,1)S(1)}, bf16[4,4,1,128,128]{4,3,1,2,0:T(8,128)(2...) while((s32[]{:T(128)}, ...), condition=%wide.region_13.14_spmd.clone.clone, body=%wide.region_10.13_spmd.clone.clone.sunk | while | flops 274532352 | bytes 33842396 | solution.py:171
  381.3 1.4 constant_dynamic-slice_fusion.10
  384.8 3.1 fusion.76
  393.6 1.4 constant_dynamic-slice_fusion.10
  397.1 3.1 fusion.76
  405.9 1.4 constant_dynamic-slice_fusion.10
  409.4 3.1 fusion.76
  421.7 3.1 fusion.76
  429.5 1.9 fusion.37
  431.4 139.7 %all-gather.2.cloned.1.call-done = bf16[4096,2048]{1,0:T(8,128)(2,1)} async-done(((bf16[512,2048]{1,0:T(8,128)(2,1)}), bf16[4096,2048]{1,0:T(8,128)(2,1)}) %all-gather.2.cloned.1.call-update) | async-done | bytes 16777232 | tf_op jit(solution)/shard_map/all_gather | solution.py:202
  571.1 12.5 %fusion.22 = bf16[4096,128]{0,1:T(8,128)(2,1)} fusion(bf16[128,2048]{0,1:T(8,128)(2,1)S(1)} %fusion.37, bf16[4096,2048]{1,0:T(8,128)(2,1)} %all-gather.2.cloned.1.call-done), kind=kOutput, calls=%fused_computation.43 | convolution fusion | flops 2148007936 | bytes 18350080 | tf_op jit(solution)/shard_map/dot_general | solution.py:201
  583.6 6.9 %reduce-scatter.2.cloned.1.call-done = bf16[2048,128]{0,1:T(8,128)(2,1)} async-done(((bf16[4096,128]{0,1:T(8,128)(2,1)}), bf16[2048,128]{0,1:T(8,128)(2,1)}) %reduce-scatter.2.cloned.1.call-update) | async-done | bytes 524304 | tf_op jit(solution)/shard_map/reduce_scatter | solution.py:207
  (175 shorter events, 56.7 us)
Async XLA Ops:
  6.5 182.3 %copy-start = (s32[8,32,3]{1,0,2:T(8,128)S(1)}, s32[8,32,3]{1,0,2:T(8,128)}, u32[]{:S(2)}) copy-start(s32[8,32,3]{1,0,2:T(8,128)} %param.18) | copy-start | bytes 9220
  6.5 2.9 copy-start.6
  6.5 137.5 %all-reduce.6.cloned.1.call-start = ((), (), s32[]{:S(2)}) async-start(), calls=%async_computation.5 | async-start | bytes 6291456 | tf_op jit(solution)/shard_map/psum | solution.py:14
  7.9 183.0 %copy-start.2 = (bf16[128,2048]{0,1:T(8,128)(2,1)}, bf16[128,2048]{0,1:T(8,128)(2,1)S(1)}, u32[]{:S(2)}) copy-start(bf16[128,2048]{0,1:T(8,128)(2,1)S(1)} %copy.84) | copy-start | bytes 1572868
  9.4 182.5 %copy-start.4 = (bf16[128,2048]{0,1:T(8,128)(2,1)}, bf16[128,2048]{0,1:T(8,128)(2,1)S(1)}, u32[]{:S(2)}) copy-start(bf16[128,2048]{0,1:T(8,128)(2,1)S(1)} %copy.85) | copy-start | bytes 1572868
  11.7 359.5 %all-reduce.4.cloned.1.call-start = ((), (), s32[]{:S(2)}) async-start(), calls=%async_computation.2 | async-start | bytes 4194304 | tf_op jit(solution)/shard_map/psum | solution.py:190
  188.1 382.9 %all-gather.2.cloned.1.call-start = ((), (), s32[]{:S(2)}) async-start(), calls=%async_computation.3 | async-start | bytes 18874368 | tf_op jit(solution)/shard_map/all_gather | solution.py:202
  197.2 4.6 copy-start.3
  197.2 4.6 copy-start.5
  197.2 178.2 %all-to-all-start = ((bf16[8,6,2,128,128]{4,3,2,1,0:T(8,128)(2,1)}), bf16[8,6,2,128,128]{4,3,2,1,0:T(8,128)(2,1)}, u32[]{:S(2)}, u32[]{:S(2)}) async-start(bf16[8,6,2,128,128]{4,3,2,1,0:T(8,128)(2,1)} %bitcast.194), calls=%async_computation | async-start | bytes 6291456 | tf_op jit(solution)/shard_map/all_to_all | solution.py:79
  201.7 388.7 %reduce-scatter.2.cloned.1.call-start = ((), (), s32[]{:S(2)}) async-start(), calls=%async_computation.4 | async-start | bytes 1572864 | tf_op jit(solution)/shard_map/reduce_scatter | solution.py:207
  202.9 45.9 %collective-permute-start = (bf16[2,128,2048]{1,2,0:T(8,128)(2,1)}, bf16[2,128,2048]{1,2,0:T(8,128)(2,1)}, u32[]{:S(2)}, u32[]{:S(2)}) collective-permute-start(bf16[2,128,2048]{1,2,0:T(8,128)(2,1)} %pad_maximum_fusion.4), channel_id=1, source_target_pairs={{0,2},{2,4},{4,6},{6,8},{8,10},{10,12},{12,14},{1,3},{3,5},{5,7},{... | collective-permute-start | bytes 3145736 | tf_op jit(solution)/shard_map/ppermute | solution.py:24
  207.6 41.2 %collective-permute-start.1 = (bf16[2,128,2048]{1,2,0:T(8,128)(2,1)}, bf16[2,128,2048]{1,2,0:T(8,128)(2,1)}, u32[]{:S(2)}, u32[]{:S(2)}) collective-permute-start(bf16[2,128,2048]{1,2,0:T(8,128)(2,1)} %pad_maximum_fusion.4), channel_id=1, source_target_pairs={{2,0},{4,2},{6,4},{8,6},{10,8},{12,10},{14,12},{3,1},{5,3},{7,5},{... | collective-permute-start | bytes 3145736 | tf_op jit(solution)/shard_map/ppermute | solution.py:25
  259.7 2.3 copy-start.7
  389.7 1.6 copy-start.8
  402.0 1.6 copy-start.8
  414.3 1.6 copy-start.8
  426.6 1.6 copy-start.8
  571.1 19.4 %copy-start.1 = (s32[8,32,3]{1,0,2:T(8,128)S(1)}, s32[8,32,3]{1,0,2:T(8,128)}, u32[]{:S(2)}) copy-start(s32[8,32,3]{1,0,2:T(8,128)} %param.18) | copy-start | bytes 9220
Sparse Core Ops, SparseCore 0:
  11.8 132.1 all-reduce.5
  188.3 152.7 all-reduce.3
  343.4 227.6 all-gather.1
  583.7 6.7 reduce-scatter.1
where the time goes:
time: 599 us; the launch traced here: 597 us
  waiting for transfers between devices  315 us (53%)
  blocking collectives  137 us (23%)
  local copies, waits for them, and re-layouts  73.9 us (12%)
  matrix products  31.6 us (5%)
  other arithmetic  14.8 us (2%)
  between operations  13.4 us (2%)
  starting transfers between devices  10.7 us (2%)
    all_gather x1, waiting for transfers between devices, local(): lax.all_gather(out_weight, 'seq', axis=0, tiled=True)  140 us
    psum x1, waiting for transfers between devices, broadcast(): return lax.psum(block, axis)  132 us
    psum x1, blocking collectives, local(): numer_terms, denoms = lax.psum((numer_terms, denoms), 'seq')  102 us
    ppermute x1, waiting for transfers between devices, padded(): before = lax.ppermute(last, axis, up)  35.9 us
    pmax x1, blocking collectives, local(): row_peak = lax.pmax(local_peak, 'seq')  35.1 us
    dot_general x1, matrix products, local(): lax.dot_general(lax.all_gather(out_weight, 'seq', axis=0, tiled=True), at...  12.5 us
    sub x4, matrix products, masked_softmax(): expon_terms = jnp.where(allowed, jnp.exp(masked - row_peak), 0.0)  12.3 us
  transfers between devices with their start and end apart: 7, of which 4 were waited for; matrix products, arithmetic and copies ran while one was open for 15% of the time, Pallas kernels for 0%

commit v1 on v0

--- a/solution.py
+++ b/solution.py
@@ -3,10 +3,23 @@
 import jax.numpy as jnp
 from jax import lax
 from jax.sharding import PartitionSpec as P
+from jax.lax import axis_index, axis_size, ppermute
 
 HD = 128
 BLK = 128
 R = 3
+
+
+def group_zone(mine_x, bus_axis):
+    top, tall = (axis_size(bus_axis), axis_index(bus_axis))
+    front, answer = (mine_x, 1)
+    while answer < top:
+        formed = ppermute(front, bus_axis, tuple(((p, p ^ answer) for p in range(top))))
+        parts_out = jnp.concatenate([front, formed], 0)
+        near = jnp.concatenate([formed, front], 0)
+        front = jnp.where(tall & answer == 0, parts_out, near)
+        answer = 2 * answer
+    return front
 
 
 def broadcast(block, axis, owner):
@@ -199,7 +212,7 @@
     tail_block = jnp.where(seq_index == seq_count - 1, glob_out[BLK:], attended)
     attended = attended.at[tokens - BLK :].set(tail_block)
     partial_terms = lax.dot_general(
-        lax.all_gather(out_weight, "seq", axis=0, tiled=True),
+        group_zone(out_weight, "seq"),
         attended,
         (((1,), (1,)), ((), ())),
         preferred_element_type=jnp.float32,

time: 599 us -> 818 us (1.37)
  waiting for transfers between devices: 315 us -> 564 us
  blocking collectives: 137 us -> 81.7 us
  other arithmetic: 14.8 us -> 28.1 us
    ppermute x0 -> x3, waiting for transfers between devices: none -> 356 us  [group_zone(): ppermute(front, bus_axis, tuple(((p, p ^ answer) for p in range(top))))]
    all_gather x1 -> x0, waiting for transfers between devices: 140 us -> none  [local(): lax.all_gather(out_weight, 'seq', axis=0, tiled=True)]
    psum x1, blocking collectives: 102 us -> 33.4 us  [local(): numer_terms, denoms = lax.psum((numer_terms, denoms), 'seq')]
    psum x1, waiting for transfers between devices: 0.01 us -> 44.3 us  [local(): numer_terms, denoms = lax.psum((numer_terms, denoms), 'seq')]
    ppermute x1, waiting for transfers between devices: 35.9 us -> 0.01 us  [padded(): before = lax.ppermute(last, axis, up)]
    psum x1, waiting for transfers between devices: 132 us -> 156 us  [broadcast(): return lax.psum(block, axis)]
    select_n x0 -> x2, other arithmetic: none -> 15.3 us  [group_zone(): front = jnp.where(tall & answer == 0, parts_out, near)]
    pmax x1, blocking collectives: 35.1 us -> 48.3 us  [local(): row_peak = lax.pmax(local_peak, 'seq')]
  transfers between devices with their start and end apart: 7 -> 9, of which waited for: 4 -> 5; matrix products, arithmetic and copies ran while one was open for 15% -> 14% of each run, Pallas kernels for 0% -> 0%
where the time goes in v1:
time: 818 us; the launch traced here: 817 us
  waiting for transfers between devices  564 us (69%)
  blocking collectives  81.7 us (10%)
  local copies, waits for them, and re-layouts  72.2 us (9%)
  matrix products  39 us (5%)
  other arithmetic  28.1 us (3%)
  starting transfers between devices  17.5 us (2%)
  between operations  13.4 us (2%)
    ppermute x3, waiting for transfers between devices, group_zone(): ppermute(front, bus_axis, tuple(((p, p ^ answer) for p in range(top))))  356 us
    psum x1, waiting for transfers between devices, broadcast(): return lax.psum(block, axis)  156 us
    pmax x1, blocking collectives, local(): row_peak = lax.pmax(local_peak, 'seq')  48.3 us
    psum x1, waiting for transfers between devices, local(): numer_terms, denoms = lax.psum((numer_terms, denoms), 'seq')  44.3 us
    psum x1, blocking collectives, local(): numer_terms, denoms = lax.psum((numer_terms, denoms), 'seq')  33.4 us
  transfers between devices with their start and end apart: 9, of which 5 were waited for; matrix products, arithmetic and copies ran while one was open for 14% of the time, Pallas kernels for 0%

profile of v1, /device:TPU:0, one launch (start us, length us, event | category | flops | bytes accessed | tf_op | source)
XLA Modules:
  0.0 816.9 jit_solution(15466783843805708800)
XLA Ops:
  6.5 3.0 collective-permute-start
  13.5 1.9 broadcast_select_fusion
  18.3 2.8 gather_fusion.2
  21.1 5.1 all-to-all-start
  28.6 5.5 collective-permute-start.3
  35.6 49.7 %collective-permute-done = bf16[512,2048]{1,0:T(8,128)(2,1)} collective-permute-done((bf16[512,2048]{1,0:T(8,128)(2,1)}, bf16[512,2048]{1,0:T(8,128)(2,1)}, u32[]{:S(2)}, u32[]{:S(2)}) %collective-permute-start) | collective-permute-done | bytes 2097184 | tf_op jit(solution)/shard_map/ppermute | solution.py:17
  85.3 5.3 maximum_select_fusion.5
  91.0 155.5 %all-reduce.6.cloned.1.call-done = (bf16[3,128,2048]{1,2,0:T(8,128)(2,1)}, bf16[3,128,2048]{1,2,0:T(8,128)(2,1)}) async-done(((bf16[3,128,2048]{1,2,0:T(8,128)(2,1)}, bf16[3,128,2048]{1,2,0:T(8,128)(2,1)}), (bf16[3,128,2048]{1,2,0:T(8,128)(2,1)}, bf16[3,128,2048]{1,2,0:T(8,128)(2,1)})) %all-reduce.6.cloned.1.call-update) | async-done | bytes 3145744 | tf_op jit(solution)/shard_map/psum | solution.py:27
  252.5 48.3 %pmax.7 = f32[16,256]{1,0:T(8,128)S(1)} all-reduce(f32[16,256]{1,0:T(8,128)S(1)} %get-tuple-element.247), channel_id=1, replica_groups=mesh['rep'=2,'seq'=8,'head'=2] {'seq'}, use_global_device_ids=true, to_apply=%region_3.4 | all-reduce | flops 4096 | bytes 32768 | tf_op jit(solution)/shard_map/pmax | solution.py:197
  300.8 3.0 fusion.32
  307.1 3.2 pad_maximum_fusion.2
  310.2 4.7 copy.103
  314.9 2.9 copy.132
  317.9 2.2 fusion.66
  326.0 33.4 %psum.31 = f32[16,256]{1,0:T(8,128)S(1)} all-reduce(f32[16,256]{1,0:T(8,128)S(1)} %fusion.31), channel_id=1, replica_groups=mesh['rep'=2,'seq'=8,'head'=2] {'seq'}, use_global_device_ids=true, to_apply=%region_6.7 | all-reduce | flops 4096 | bytes 32768 | tf_op jit(solution)/shard_map/psum | solution.py:203
  359.4 44.3 %all-reduce.4.cloned.1.call-done = f32[16,256,128]{2,1,0:T(8,128)} async-done(((f32[16,256,128]{2,1,0:T(8,128)}), f32[16,256,128]{2,1,0:T(8,128)}) %all-reduce.4.cloned.1.call-update) | async-done | bytes 2097168 | tf_op jit(solution)/shard_map/psum | solution.py:203
  407.9 3.0 gather_fusion.3
  413.2 10.0 %maximum_select_fusion.2 = bf16[2048,2048]{1,0:T(8,128)(2,1)} fusion(bf16[1024,2048]{1,0:T(8,128)(2,1)} %collective-permute-done.1, bf16[1024,2048]{1,0:T(8,128)(2,1)} %maximum_select_fusion.5, pred[]{:T(512)S(6)} %eq.79), kind=kLoop, calls=%fused_computation.50 | loop fusion | flops 37748736 | bytes 16777216 | tf_op jit(solution)/shard_map/jit(_where)/select_n | solution.py:20
  423.2 2.1 collective-permute-start.2
  425.3 53.2 %while.16 = (s32[]{:T(128)}, bf16[4,4,1,128,128]{3,4,1,0,2:T(8,128)(2,1)}, pred[4,4,1,1024]{3,1,2,0:T(4,128)(4,1)}, bf16[4,4,1,128,128]{4,3,1,2,0:T(8,128)(2,1)}...) while((s32[]{:T(128)}, ...), condition=%wide.region_13.14_spmd.clone.clone, body=%wide.region_10.13_spmd.clone.clone.sunk | while | flops 274532352 | bytes 25452752 | solution.py:184
  432.7 3.1 fusion.83
  435.8 2.1 fusion.84
  446.0 3.1 fusion.83
  449.0 2.1 fusion.84
  459.3 3.1 fusion.83
  462.3 2.1 fusion.84
  472.5 3.1 fusion.83
  475.6 2.1 fusion.84
  479.8 306.3 %collective-permute-done.2 = bf16[2048,2048]{1,0:T(8,128)(2,1)} collective-permute-done((bf16[2048,2048]{1,0:T(8,128)(2,1)}, bf16[2048,2048]{1,0:T(8,128)(2,1)}, u32[]{:S(2)}, u32[]{:S(2)}) %collective-permute-start.2) | collective-permute-done | bytes 8388640 | tf_op jit(solution)/shard_map/ppermute | solution.py:17
  786.1 13.5 %fusion.29 = bf16[4096,128]{1,0:T(8,128)(2,1)} fusion(bf16[128,2048]{0,1:T(8,128)(2,1)S(1)} %fusion.44, bf16[2048,2048]{1,0:T(8,128)(2,1)} %collective-permute-done.2, bf16[2048,2048]{1,0:T(8,128)(2,1)} %maximum_select_fusion.2, pred[]{:T(512)S(6)} %eq.78), kind=kOutput, calls=%fused_computation.51 | convolution fusion | flops 2223505408 | bytes 18350080 | tf_op jit(solution)/shard_map/dot_general | solution.py:214
  799.6 8.7 %reduce-scatter.2.cloned.1.call-done = bf16[2048,128]{1,0:T(8,128)(2,1)} async-done(((bf16[4096,128]{1,0:T(8,128)(2,1)}), bf16[2048,128]{1,0:T(8,128)(2,1)}) %reduce-scatter.2.cloned.1.call-update) | async-done | bytes 524304 | tf_op jit(solution)/shard_map/reduce_scatter | solution.py:220
  808.3 2.0 copy.121
  (167 shorter events, 65.8 us)
Async XLA Ops:
  6.5 8.9 %copy-start = (s32[8,32,3]{1,0,2:T(8,128)S(1)}, s32[8,32,3]{1,0,2:T(8,128)}, u32[]{:S(2)}) copy-start(s32[8,32,3]{1,0,2:T(8,128)} %param.18) | copy-start | bytes 9220
  6.5 239.9 %all-reduce.6.cloned.1.call-start = ((), (), s32[]{:S(2)}) async-start(), calls=%async_computation.4 | async-start | bytes 6291456 | tf_op jit(solution)/shard_map/psum | solution.py:27
  6.5 78.7 %collective-permute-start = (bf16[512,2048]{1,0:T(8,128)(2,1)}, bf16[512,2048]{1,0:T(8,128)(2,1)}, u32[]{:S(2)}, u32[]{:S(2)}) collective-permute-start(bf16[512,2048]{1,0:T(8,128)(2,1)} %param.19), channel_id=1, source_target_pairs={{0,2},{2,0},{4,6},{6,4},{8,10},{10,8},{12,14},{14,12},{1,3},{3,1},... | collective-permute-start | bytes 6291464 | tf_op jit(solution)/shard_map/ppermute | solution.py:17
  21.1 64.2 %copy-start.3 = (bf16[512,2048]{1,0:T(8,128)(2,1)S(1)}, bf16[512,2048]{1,0:T(8,128)(2,1)}, u32[]{:S(2)}) copy-start(bf16[512,2048]{1,0:T(8,128)(2,1)} %param.19) | copy-start | bytes 6291460
  21.1 386.8 %all-to-all-start = ((bf16[8,6,2,128,128]{4,3,2,1,0:T(8,128)(2,1)}), bf16[8,6,2,128,128]{4,3,2,1,0:T(8,128)(2,1)}, u32[]{:S(2)}, u32[]{:S(2)}) async-start(bf16[8,6,2,128,128]{4,3,2,1,0:T(8,128)(2,1)} %bitcast.191), calls=%async_computation | async-start | bytes 6291456 | tf_op jit(solution)/shard_map/all_to_all | solution.py:92
  26.2 377.4 %all-reduce.4.cloned.1.call-start = ((), (), s32[]{:S(2)}) async-start(), calls=%async_computation.2 | async-start | bytes 4194304 | tf_op jit(solution)/shard_map/psum | solution.py:203
  27.3 279.7 %collective-permute-start.4 = (bf16[2,128,2048]{1,2,0:T(8,128)(2,1)}, bf16[2,128,2048]{1,2,0:T(8,128)(2,1)}, u32[]{:S(2)}, u32[]{:S(2)}) collective-permute-start(bf16[2,128,2048]{1,2,0:T(8,128)(2,1)} %pad_maximum_fusion.4), channel_id=1, source_target_pairs={{2,0},{4,2},{6,4},{8,6},{10,8},{12,10},{14,12},{3,1},{5,3},{7,5},{... | collective-permute-start | bytes 3145736 | tf_op jit(solution)/shard_map/ppermute | solution.py:38
  28.6 278.4 %collective-permute-start.3 = (bf16[2,128,2048]{1,2,0:T(8,128)(2,1)}, bf16[2,128,2048]{1,2,0:T(8,128)(2,1)}, u32[]{:S(2)}, u32[]{:S(2)}) collective-permute-start(bf16[2,128,2048]{1,2,0:T(8,128)(2,1)} %pad_maximum_fusion.4), channel_id=1, source_target_pairs={{0,2},{2,4},{4,6},{6,8},{8,10},{10,12},{12,14},{1,3},{3,5},{5,7},{... | collective-permute-start | bytes 3145736 | tf_op jit(solution)/shard_map/ppermute | solution.py:37
  90.6 322.6 %collective-permute-start.1 = (bf16[1024,2048]{1,0:T(8,128)(2,1)}, bf16[1024,2048]{1,0:T(8,128)(2,1)}, u32[]{:S(2)}, u32[]{:S(2)}) collective-permute-start(bf16[1024,2048]{1,0:T(8,128)(2,1)} %maximum_select_fusion.5), channel_id=1, source_target_pairs={{0,4},{2,6},{4,0},{6,2},{8,12},{10,14},{12,8},{14,10},{1,5},{3,7},... | collective-permute-start | bytes 12582920 | tf_op jit(solution)/shard_map/ppermute | solution.py:17
  303.9 504.5 %reduce-scatter.2.cloned.1.call-start = ((), (), s32[]{:S(2)}) async-start(), calls=%async_computation.3 | async-start | bytes 1572864 | tf_op jit(solution)/shard_map/reduce_scatter | solution.py:220
  317.8 2.2 copy-start.4
  423.2 362.9 %collective-permute-start.2 = (bf16[2048,2048]{1,0:T(8,128)(2,1)}, bf16[2048,2048]{1,0:T(8,128)(2,1)}, u32[]{:S(2)}, u32[]{:S(2)}) collective-permute-start(bf16[2048,2048]{1,0:T(8,128)(2,1)} %maximum_select_fusion.2), channel_id=1, source_target_pairs={{0,8},{2,10},{4,12},{6,14},{8,0},{10,2},{12,4},{14,6},{1,9},{3,11}... | collective-permute-start | bytes 25165832 | tf_op jit(solution)/shard_map/ppermute | solution.py:17
  425.3 53.2 %copy-start.2 = (bf16[128,16,128]{0,2,1:T(8,128)(2,1)S(1)}, bf16[128,16,128]{0,2,1:T(8,128)(2,1)}, u32[]{:S(2)}) copy-start(bf16[128,16,128]{0,2,1:T(8,128)(2,1)} %copy.94) | copy-start | bytes 1572868
  786.1 24.2 %copy-start.1 = (s32[8,32,3]{1,0,2:T(8,128)S(1)}, s32[8,32,3]{1,0,2:T(8,128)}, u32[]{:S(2)}) copy-start(s32[8,32,3]{1,0,2:T(8,128)} %param.18) | copy-start | bytes 9220
Sparse Core Ops, SparseCore 0:
  15.6 230.8 all-reduce.5
  304.0 99.6 all-reduce.3
  799.7 8.5 reduce-scatter.1
